TPU v7x, 256 devices: a whole 4x4x8 slice. The times are simulated.
256 devices in a mesh: row: 16 (over x, y_hi, core), col: 16 (over y_lo, z).
Axes of the slice: x: 4, y: 4 (y_hi: 2, y_lo: 2; y = y_hi * 2 + y_lo), z: 8, core: 2. Of those that a mesh axis runs over, the one named last changes fastest.
Arguments:
- query_in: bfloat16 [4096, 8192], P('row', 'col'), may hold values from -6 to 6
- key_in: bfloat16 [4096, 8192], P('row', 'col'), may hold values from -6 to 6
- value_in: bfloat16 [4096, 8192], P('row', 'col'), may hold values from -6 to 6
- filters: float32 [512, 128], P('col'), may hold values from -0.5 to 0.5
- out_weight: bfloat16 [8192, 8192], P('row', 'col'), may hold values from -0.0625 to 0.0625
- out_grad: bfloat16 [4096, 8192], P('row', 'col'), may hold values from -6 to 6
Outputs:
- mixed: bfloat16 [4096, 8192], P('row', 'col')
- query_grad: bfloat16 [4096, 8192], P('row', 'col')
- key_grad: bfloat16 [4096, 8192], P('row', 'col')
- value_grad: bfloat16 [4096, 8192], P('row', 'col')
- weight_grad: bfloat16 [8192, 8192], P('row', 'col')
- filter_grad: float32 [512, 128], P('col')
All inputs are finite; a program needn't handle non-finite values.
Results may differ from a plain program's by a relative error of at most 0.018.
Values may be sent and summed in bfloat16 or wider, within the bound.
A program may use at most 128 MiB of HBM per device.

v0:
```python
import math
import jax
import jax.numpy as jnp
from jax import lax
from jax.sharding import PartitionSpec as P


def from_behind(shard, axis, by):
    size = lax.axis_size(axis)
    pairs = [(i, i + by) for i in range(size) if 0 <= i + by < size]
    return lax.ppermute(shard, axis, pairs)


def toeplitz(taps, causal):
    groups, span = taps.shape
    if causal:
        template = jnp.concatenate(
            [
                jnp.zeros((groups, 1), jnp.float32),
                taps[:, ::-1],
                jnp.zeros((groups, span), jnp.float32),
            ],
            1,
        )
    else:
        template = jnp.concatenate([taps, jnp.zeros((groups, span + 1), jnp.float32)], 1)
    tiled = jnp.tile(template, (1, span))
    return tiled[:, : 2 * span * span].reshape(groups, span, 2 * span)


def windows(extended, span):
    count = (extended.shape[0] - span) // span
    first = extended[:-span].reshape(count, span, extended.shape[1])
    second = extended[span:].reshape(count, span, extended.shape[1])
    return jnp.concatenate([first, second], axis=1)


def convolve(matrix, extended, span, group):
    blocks = windows(extended, span)
    count, _, width = blocks.shape
    split = blocks.reshape(count, 2 * span, width // group, group)
    result = jnp.einsum("gts,bsgc->btgc", matrix, split, precision=lax.Precision.HIGHEST)
    return result.reshape(count * span, width)


def shards(query_in, key_in, value_in, filters, out_weight, out_grad):
    f32 = jnp.float32
    bf16 = jnp.bfloat16
    tokens, width = query_in.shape
    span = filters.shape[1]
    group = width // filters.shape[0]
    total_tokens = tokens * lax.axis_size("row")
    key32 = key_in.astype(f32)
    value32 = value_in.astype(f32)
    query32 = query_in.astype(f32)
    product = key32 * value32
    key_rim, value_rim = from_behind((key_in[-span:], value_in[-span:]), "row", 1)
    product_rim = key_rim.astype(f32) * value_rim.astype(f32)
    product_ext = jnp.concatenate([product_rim, product], 0)
    conv = convolve(toeplitz(filters, True), product_ext, span, group)
    gated = (query32 * conv).astype(bf16)
    panel = lax.all_gather(gated, "col", axis=1, tiled=True)
    weights = lax.all_gather(out_weight, "row", axis=0, tiled=True)
    mixed_sum = jnp.dot(panel, weights, preferred_element_type=f32)
    partial_value = lax.dot_general(
        out_grad, weights, (((1,), (1,)), ((), ())), preferred_element_type=f32
    )
    mixed = mixed_sum.astype(bf16)
    grad_gated = lax.psum_scatter(
        partial_value.astype(jnp.bfloat16), "col", scatter_dimension=1, tiled=True
    ).astype(jnp.float32)
    query_grad = (grad_gated * conv).astype(bf16)
    grad_conv = grad_gated * query32
    grad_rim = from_behind(grad_conv[:span].astype(jnp.bfloat16), "row", -1).astype(jnp.float32)
    grad_ext = jnp.concatenate([grad_conv, grad_rim], 0)
    grad_product = convolve(toeplitz(filters, False), grad_ext, span, group)
    key_grad = (grad_product * value32).astype(bf16)
    value_grad = (grad_product * key32).astype(bf16)
    count = tokens // span
    groups = width // group
    grad_blocks = grad_conv.reshape(count, span, groups, group)
    product_blocks = windows(product_ext, span).reshape(count, 2 * span, groups, group)
    corr = jnp.einsum(
        "btgc,bsgc->gts", grad_blocks, product_blocks, precision=lax.Precision.HIGHEST
    )
    flat = jnp.concatenate(
        [corr.reshape(groups, 2 * span * span), jnp.zeros((groups, span), f32)], 1
    )
    skewed = flat.reshape(groups, span, 2 * span + 1)[:, :, 1 : span + 1]
    local_taps = jnp.sum(skewed, axis=1)[:, ::-1]
    filter_grad = lax.psum(local_taps, "row") * (1.0 / math.sqrt(total_tokens * group))
    weight_sum = lax.psum_scatter(
        lax.dot_general(
            panel, out_grad, (((0,), (0,)), ((), ())), preferred_element_type=f32
        ).astype(jnp.bfloat16),
        "row",
        scatter_dimension=0,
        tiled=True,
    ).astype(jnp.float32)
    weight_grad = (weight_sum * (1.0 / math.sqrt(total_tokens))).astype(bf16)
    return (mixed, query_grad, key_grad, value_grad, weight_grad, filter_grad)


def solution(mesh):
    placed = (
        P("row", "col"),
        P("row", "col"),
        P("row", "col"),
        P("col", None),
        P("row", "col"),
        P("row", "col"),
    )
    return jax.shard_map(
        shards,
        mesh=mesh,
        in_specs=placed,
        out_specs=(
            P("row", "col"),
            P("row", "col"),
            P("row", "col"),
            P("row", "col"),
            P("row", "col"),
            P("col", None),
        ),
        check_vma=False,
    )
```

profile of v0, /device:TPU:2, one launch (start us, length us, event | category | flops | bytes accessed | tf_op | source)
XLA Modules:
  0.0 399.6 jit_solution(14120310710008545654)
XLA Ops:
  7.2 0.0 copy-start
  7.2 0.0 all-gather.5.cloned.1.call-start
  7.2 0.7 all-gather.5.cloned.1.call-update
  7.9 0.0 reduce-scatter.3.cloned.1.call-start
  8.0 82.3 %all-gather.5.cloned.1.call-done = bf16[8192,512]{1,0:T(8,128)(2,1)} async-done(((bf16[512,512]{1,0:T(8,128)(2,1)}), bf16[8192,512]{1,0:T(8,128)(2,1)}) %all-gather.5.cloned.1.call-update) | async-done | bytes 8388624 | tf_op jit(solution)/shard_map/all_gather | solution.py:63
  90.2 7.8 %convolution_convert_fusion.1 = bf16[256,8192]{1,0:T(8,128)(2,1)} fusion(bf16[256,512]{1,0:T(8,128)(2,1)S(1)} %copy-done, bf16[8192,512]{1,0:T(8,128)(2,1)} %all-gather.5.cloned.1.call-done), kind=kOutput, calls=%fused_computation.1 | convolution fusion | flops 2149580800 | bytes 12845056 | tf_op jit(solution)/shard_map/dot_general | solution.py:65
  98.1 0.0 reduce-scatter.3.cloned.1.call-update
  98.1 0.0 all-gather.3.cloned.1.call-start
  98.1 0.9 copy-done.6
  99.0 0.1 copy.15
  99.2 2.1 collective-permute-start
  101.3 0.1 copy.16
  101.5 2.3 collective-permute-start.1
  103.8 0.1 rev.6
  103.9 3.1 tile.20
  107.0 6.7 %tile.21 = f32[32,32896]{1,0:T(8,128)} reshape(f32[32,128,257]{2,1,0:T(8,128)} %tile.20) | data formatting | bytes 8421376 | tf_op jit(solution)/shard_map/tile | solution.py:27
  113.7 2.2 slice-done
  115.9 3.3 copy.37
  119.2 0.1 pad.8.clone
  119.3 0.1 maximum_maximum_fusion
  119.4 3.1 tile.8
  122.5 6.7 %tile.9 = f32[32,32896]{1,0:T(8,128)} reshape(f32[32,128,257]{2,1,0:T(8,128)} %tile.8) | data formatting | bytes 8421376 | tf_op jit(solution)/shard_map/tile | solution.py:27
  129.2 2.2 slice-done.1
  131.4 3.2 copy.35
  134.6 44.5 %reduce-scatter.3.cloned.1.call-done = bf16[256,512]{1,0:T(8,128)(2,1)} async-done(((bf16[256,8192]{1,0:T(8,128)(2,1)}), bf16[256,512]{1,0:T(8,128)(2,1)}) %reduce-scatter.3.cloned.1.call-update) | async-done | bytes 262160 | tf_op jit(solution)/shard_map/reduce_scatter | solution.py:69
  179.1 1.0 convert_multiply_fusion
  180.2 0.7 slice.42
  180.8 2.1 collective-permute-start.2
  182.9 0.0 collective-permute-done
  182.9 0.0 collective-permute-done.1
  183.0 0.2 copy.24
  183.2 0.3 concatenate.37
  183.5 2.0 collective-permute-done.2
  185.6 0.2 copy.25
  185.8 0.3 concatenate.39
  186.2 5.9 %fusion.7 = f32[2,128,32,16]{1,3,0,2:T(8,128)S(1)} fusion(f32[32,128,256,1]{2,1,0,3:T(8,128)} %bitcast.60, f32[2,128,32,16]{1,3,0,2:T(8,128)S(1)} %copy.27, f32[2,128,32,16]{1,3,0,2:T(8,128)S(1)} %copy.26), kind=kOutput, calls=%fused_computation.8 | convolution fusion | flops 402915328 | bytes 5767168 | tf_op jit(solution)/shard_map/gts,bsgc->btgc/dot_general | solution.py:42
  192.1 0.3 copy.28
  192.4 0.9 fusion.14
  193.3 0.3 concatenate.34
  193.6 0.3 concatenate.33
  193.9 0.1 copy_dynamic-update-slice_fusion.1
  193.9 0.1 copy_dynamic-update-slice_fusion
  194.0 5.9 %fusion.4 = f32[2,128,32,16]{1,3,0,2:T(8,128)S(1)} fusion(f32[2,256,32,16]{1,3,0,2:T(8,128)S(1)} %copy_dynamic-update-slice_fusion, f32[32,128,256,1]{2,1,0,3:T(8,128)} %bitcast.59), kind=kOutput, calls=%fused_computation.7 | convolution fusion | flops 402653184 | bytes 5767168 | tf_op jit(solution)/shard_map/gts,bsgc->btgc/dot_general | solution.py:42
  200.0 0.3 copy.21
  200.3 0.2 copy.22
  200.5 0.9 fusion.16
  201.4 0.0 all-gather.3.cloned.1.call-update
  201.4 0.3 reduce-scatter.5.cloned.1.call-start
  201.7 73.7 %all-gather.3.cloned.1.call-done = bf16[256,8192]{1,0:T(8,128)(2,1)} async-done(((bf16[256,512]{1,0:T(8,128)(2,1)}), bf16[256,8192]{1,0:T(8,128)(2,1)}) %all-gather.3.cloned.1.call-update) | async-done | bytes 4194320 | tf_op jit(solution)/shard_map/all_gather | solution.py:62
  275.4 7.8 %convolution_convert_fusion = bf16[8192,512]{1,0:T(8,128)(2,1)} fusion(bf16[256,8192]{1,0:T(8,128)(2,1)} %all-gather.3.cloned.1.call-done, bf16[256,512]{1,0:T(8,128)(2,1)S(1)} %copy-done), kind=kOutput, calls=%fused_computation | convolution fusion | flops 2151677952 | bytes 12845056 | tf_op jit(solution)/shard_map/dot_general | solution.py:93
  283.2 0.0 reduce-scatter.5.cloned.1.call-update
  283.2 3.5 fusion.18
  286.7 2.4 copy.39
  289.2 2.3 concatenate.42
  291.5 8.2 %reshape.61 = f32[32,128,257]{2,1,0:T(8,128)} reshape(f32[32,32896]{1,0:T(8,128)} %concatenate.42) | data formatting | bytes 8421376 | tf_op jit(solution)/shard_map/reshape | solution.py:89
  299.7 3.2 slice_reduce_fusion
  303.0 0.1 rev.7
  303.0 0.8 copy.30
  303.9 0.8 copy.31
  304.7 57.5 %psum.7 = f32[32,128]{1,0:T(8,128)S(1)} all-reduce(f32[32,128]{1,0:T(8,128)S(1)} %rev.7), channel_id=1, replica_groups=mesh['row'=16,'col'=16] {'row'}, use_global_device_ids=true, to_apply=%region_3.0 | all-reduce | flops 4096 | bytes 32768 | tf_op jit(solution)/shard_map/psum | solution.py:91
  362.3 0.6 broadcast_multiply_fusion
  362.9 7.7 %convolution_convert_fusion.2 = bf16[256,512]{1,0:T(8,128)(2,1)} fusion(bf16[256,8192]{1,0:T(8,128)(2,1)} %all-gather.3.cloned.1.call-done, bf16[8192,512]{1,0:T(8,128)(2,1)} %all-gather.5.cloned.1.call-done), kind=kOutput, calls=%fused_computation.9 | convolution fusion | flops 2147614720 | bytes 12845056 | tf_op jit(solution)/shard_map/dot_general | solution.py:64
  370.6 20.6 %reduce-scatter.5.cloned.1.call-done = bf16[512,512]{1,0:T(8,128)(2,1)} async-done(((bf16[8192,512]{1,0:T(8,128)(2,1)}), bf16[512,512]{1,0:T(8,128)(2,1)}) %reduce-scatter.5.cloned.1.call-update) | async-done | bytes 524304 | tf_op jit(solution)/shard_map/reduce_scatter | solution.py:92
  391.2 1.9 multiply_convert_fusion
  (30 shorter events, 0.3 us)
Async XLA Ops:
  7.2 83.1 %copy-start = (bf16[256,512]{1,0:T(8,128)(2,1)S(1)}, bf16[256,512]{1,0:T(8,128)(2,1)}, u32[]{:S(2)}) copy-start(bf16[256,512]{1,0:T(8,128)(2,1)} %param.11) | copy-start | bytes 786436
  7.2 83.1 %all-gather.5.cloned.1.call-start = ((), (), s32[]{:S(2)}) async-start(), calls=%async_computation.3 | async-start | bytes 8912896 | tf_op jit(solution)/shard_map/all_gather | solution.py:63
  7.9 171.2 %reduce-scatter.3.cloned.1.call-start = ((), (), s32[]{:S(2)}) async-start(), calls=%async_computation.4 | async-start | bytes 4456448 | tf_op jit(solution)/shard_map/reduce_scatter | solution.py:69
  98.0 0.9 copy-start.6
  98.1 3.2 copy-start.7
  98.1 5.7 %copy-start.8 = (f32[32,128]{1,0:T(8,128)S(1)}, f32[32,128]{1,0:T(8,128)}, u32[]{:S(2)}) copy-start(f32[32,128]{1,0:T(8,128)} %param.9) | copy-start | bytes 49156
  98.1 177.3 %all-gather.3.cloned.1.call-start = ((), (), s32[]{:S(2)}) async-start(), calls=%async_computation.2 | async-start | bytes 4456448 | tf_op jit(solution)/shard_map/all_gather | solution.py:62
  99.2 83.8 %collective-permute-start = (bf16[128,512]{0,1:T(8,128)(2,1)S(1)}, bf16[128,512]{0,1:T(8,128)(2,1)S(1)}, u32[]{:S(2)}, u32[]{:S(2)}) collective-permute-start(bf16[128,512]{0,1:T(8,128)(2,1)S(1)} %slice.34), channel_id=1, source_target_pairs={{0,16},{16,32},{32,48},{48,64},{64,80},{80,96},{96,112},{112,128},... | collective-permute-start | bytes 393224 | tf_op jit(solution)/shard_map/ppermute | solution.py:11
  101.5 81.5 %collective-permute-start.1 = (bf16[128,512]{0,1:T(8,128)(2,1)S(1)}, bf16[128,512]{0,1:T(8,128)(2,1)S(1)}, u32[]{:S(2)}, u32[]{:S(2)}) collective-permute-start(bf16[128,512]{0,1:T(8,128)(2,1)S(1)} %slice.35), channel_id=1, source_target_pairs={{0,16},{16,32},{32,48},{48,64},{64,80},{80,96},{96,112},{112,128},... | collective-permute-start | bytes 393224 | tf_op jit(solution)/shard_map/ppermute | solution.py:11
  113.7 2.2 slice-start
  129.2 2.2 slice-start.1
  131.4 47.7 %copy-start.2 = (bf16[256,512]{1,0:T(8,128)(2,1)S(1)}, bf16[256,512]{1,0:T(8,128)(2,1)}, u32[]{:S(2)}) copy-start(bf16[256,512]{1,0:T(8,128)(2,1)} %param.6) | copy-start | bytes 786436
  180.8 4.7 %collective-permute-start.2 = (bf16[128,512]{1,0:T(8,128)(2,1)}, bf16[128,512]{1,0:T(8,128)(2,1)S(1)}, u32[]{:S(2)}, u32[]{:S(2)}) collective-permute-start(bf16[128,512]{1,0:T(8,128)(2,1)} %slice.42), channel_id=1, source_target_pairs={{16,0},{32,16},{48,32},{64,48},{80,64},{96,80},{112,96},{128,112},... | collective-permute-start | bytes 393224 | tf_op jit(solution)/shard_map/ppermute | solution.py:11
  194.0 6.5 %copy-start.3 = (bf16[256,512]{1,0:T(8,128)(2,1)S(1)}, bf16[256,512]{1,0:T(8,128)(2,1)}, u32[]{:S(2)}) copy-start(bf16[256,512]{1,0:T(8,128)(2,1)} %reduce-scatter.3.cloned.1.call-done) | copy-start | bytes 786436
  201.4 189.7 %reduce-scatter.5.cloned.1.call-start = ((), (), s32[]{:S(2)}) async-start(), calls=%async_computation.5 | async-start | bytes 8912896 | tf_op jit(solution)/shard_map/reduce_scatter | solution.py:92
  291.5 11.5 %copy-start.5 = (bf16[256,512]{0,1:T(8,128)(2,1)S(1)}, bf16[256,512]{0,1:T(8,128)(2,1)}, u32[]{:S(2)}) copy-start(bf16[256,512]{0,1:T(8,128)(2,1)} %get-tuple-element.13) | copy-start | bytes 786436
  291.5 12.4 %copy-start.4 = (bf16[256,512]{0,1:T(8,128)(2,1)S(1)}, bf16[256,512]{0,1:T(8,128)(2,1)}, u32[]{:S(2)}) copy-start(bf16[256,512]{0,1:T(8,128)(2,1)} %get-tuple-element.12) | copy-start | bytes 786436
  362.9 30.2 %copy-start.1 = (bf16[256,512]{1,0:T(8,128)(2,1)S(1)}, bf16[256,512]{1,0:T(8,128)(2,1)}, u32[]{:S(2)}) copy-start(bf16[256,512]{1,0:T(8,128)(2,1)} %param.11) | copy-start | bytes 786436
Sparse Core Ops, SparseCore 0:
  10.7 79.5 all-gather.4
  98.2 80.8 reduce-scatter.2
  201.6 73.8 all-gather.2
  283.4 107.7 reduce-scatter.4
where the time goes:
time: 400 us
  waiting for transfers between devices  224 us (56%)
  blocking collectives  57.5 us (14%)
  local copies, waits for them, and re-layouts  49.8 us (12%)
  matrix products  38.7 us (10%)
  between operations  14.1 us (4%)
  other arithmetic  8.78 us (2%)
  starting transfers between devices  6.92 us (2%)
    all_gather x1, waiting for transfers between devices, shards(): weights = lax.all_gather(out_weight, 'row', axis=0, tiled=True)  82.3 us
    all_gather x1, waiting for transfers between devices, shards(): panel = lax.all_gather(gated, 'col', axis=1, tiled=True)  73.7 us
    psum x1, blocking collectives, shards(): lax.psum(local_taps, 'row') * (1.0 / math.sqrt(total_tokens * group))  57.5 us
    reduce_scatter x1, waiting for transfers between devices, shards(): lax.psum_scatter(partial_value.astype(jnp.bfloat16), 'col', scatter_dimen...  44.5 us
    reduce_scatter x1, waiting for transfers between devices, shards(): lax.psum_scatter(lax.dot_general(panel, out_grad, (((0,), (0,)), ((), ())...  20.6 us
    another operation x4, local copies, waits for them, and re-layouts, toeplitz(): tiled = jnp.tile(template, (1, span))  19.6 us
    unnamed x27, local copies, waits for them, and re-layouts  12 us
    dot_general x2, matrix products, convolve(): jnp.einsum('gts,bsgc->btgc', matrix, split, precision=lax.Precision.HIGHEST)  11.9 us
  transfers between devices with their start and end apart: 7, of which 5 were waited for; matrix products, arithmetic and copies ran while one was open for 15% of the time, Pallas kernels for 0%

commit v1 on v0

--- a/solution.py
+++ b/solution.py
@@ -59,7 +59,9 @@
     product_ext = jnp.concatenate([product_rim, product], 0)
     conv = convolve(toeplitz(filters, True), product_ext, span, group)
     gated = (query32 * conv).astype(bf16)
-    panel = lax.all_gather(gated, "col", axis=1, tiled=True)
+    panel = jnp.concatenate(
+        lax.all_to_all(jnp.stack([gated] * lax.axis_size("col")), "col", 0, 0), axis=1
+    )
     weights = lax.all_gather(out_weight, "row", axis=0, tiled=True)
     mixed_sum = jnp.dot(panel, weights, preferred_element_type=f32)
     partial_value = lax.dot_general(

time: 400 us -> 425 us (1.062)
  blocking collectives: 57.5 us -> 157 us
  waiting for transfers between devices: 224 us -> 149 us
    all_to_all x0 -> x1, blocking collectives: none -> 95.5 us  [shards(): lax.all_to_all(jnp.stack([gated] * lax.axis_size('col')), 'col', 0, 0)]
    all_gather x1 -> x0, waiting for transfers between devices: 73.7 us -> none  [shards(): panel = lax.all_gather(gated, 'col', axis=1, tiled=True)]
  transfers between devices with their start and end apart: 7 -> 6, of which waited for: 5 -> 4; matrix products, arithmetic and copies ran while one was open for 15% -> 14% of each run, Pallas kernels for 0% -> 0%
where the time goes in v1:
time: 425 us; the launch traced here: 424 us
  blocking collectives  157 us (37%)
  waiting for transfers between devices  149 us (35%)
  local copies, waits for them, and re-layouts  52.2 us (12%)
  matrix products  36.4 us (9%)
  between operations  14.1 us (3%)
  other arithmetic  8.69 us (2%)
  starting transfers between devices  6.66 us (2%)
    all_to_all x1, blocking collectives, shards(): lax.all_to_all(jnp.stack([gated] * lax.axis_size('col')), 'col', 0, 0)  95.5 us
    all_gather x1, waiting for transfers between devices, shards(): weights = lax.all_gather(out_weight, 'row', axis=0, tiled=True)  82.3 us
    psum x1, blocking collectives, shards(): lax.psum(local_taps, 'row') * (1.0 / math.sqrt(total_tokens * group))  61.5 us
    reduce_scatter x1, waiting for transfers between devices, shards(): lax.psum_scatter(partial_value.astype(jnp.bfloat16), 'col', scatter_dimen...  44.3 us
    reduce_scatter x1, waiting for transfers between devices, shards(): lax.psum_scatter(lax.dot_general(panel, out_grad, (((0,), (0,)), ((), ())...  19.7 us
    another operation x4, local copies, waits for them, and re-layouts, toeplitz(): tiled = jnp.tile(template, (1, span))  19.6 us
    unnamed x27, local copies, waits for them, and re-layouts  14 us
    dot_general x2, matrix products, convolve(): jnp.einsum('gts,bsgc->btgc', matrix, split, precision=lax.Precision.HIGHEST)  11.9 us
  transfers between devices with their start and end apart: 6, of which 4 were waited for; matrix products, arithmetic and copies ran while one was open for 14% of the time, Pallas kernels for 0%

profile of v1, /device:TPU:2, one launch (start us, length us, event | category | flops | bytes accessed | tf_op | source)
XLA Modules:
  0.0 424.2 jit_solution(544346793753258520)
XLA Ops:
  7.2 0.0 copy-start
  7.2 0.0 all-gather.2.cloned.1.call-start
  7.2 0.7 all-gather.2.cloned.1.call-update
  7.9 0.0 reduce-scatter.3.cloned.1.call-start
  8.0 82.3 %all-gather.2.cloned.1.call-done = bf16[8192,512]{1,0:T(8,128)(2,1)} async-done(((bf16[512,512]{1,0:T(8,128)(2,1)}), bf16[8192,512]{1,0:T(8,128)(2,1)}) %all-gather.2.cloned.1.call-update) | async-done | bytes 8388624 | tf_op jit(solution)/shard_map/all_gather | solution.py:65
  90.2 7.8 %convolution_convert_fusion.1 = bf16[256,8192]{1,0:T(8,128)(2,1)} fusion(bf16[256,512]{1,0:T(8,128)(2,1)S(1)} %copy-done, bf16[8192,512]{1,0:T(8,128)(2,1)} %all-gather.2.cloned.1.call-done), kind=kOutput, calls=%fused_computation.1 | convolution fusion | flops 2149580800 | bytes 12845056 | tf_op jit(solution)/shard_map/dot_general | solution.py:67
  98.0 0.0 reduce-scatter.3.cloned.1.call-update
  98.1 0.0 reduce-scatter.5.cloned.1.call-start
  98.1 0.9 copy-done.6
  99.0 0.1 copy.15
  99.1 2.1 collective-permute-start
  101.3 0.1 copy.16
  101.5 2.3 collective-permute-start.1
  103.8 0.1 rev.6
  103.9 3.1 tile.20
  107.0 6.7 %tile.21 = f32[32,32896]{1,0:T(8,128)} reshape(f32[32,128,257]{2,1,0:T(8,128)} %tile.20) | data formatting | bytes 8421376 | tf_op jit(solution)/shard_map/tile | solution.py:27
  113.6 2.2 slice-done
  115.8 3.3 copy.38
  119.1 0.1 pad.8.clone
  119.2 0.1 maximum_maximum_fusion
  119.3 3.1 tile.8
  122.4 6.7 %tile.9 = f32[32,32896]{1,0:T(8,128)} reshape(f32[32,128,257]{2,1,0:T(8,128)} %tile.8) | data formatting | bytes 8421376 | tf_op jit(solution)/shard_map/tile | solution.py:27
  129.1 2.2 slice-done.1
  131.3 3.2 copy.36
  134.6 44.3 %reduce-scatter.3.cloned.1.call-done = bf16[256,512]{1,0:T(8,128)(2,1)} async-done(((bf16[256,8192]{1,0:T(8,128)(2,1)}), bf16[256,512]{1,0:T(8,128)(2,1)}) %reduce-scatter.3.cloned.1.call-update) | async-done | bytes 262160 | tf_op jit(solution)/shard_map/reduce_scatter | solution.py:71
  178.8 1.0 convert_multiply_fusion
  179.9 0.7 slice.42
  180.5 2.1 collective-permute-start.2
  182.6 0.0 collective-permute-done
  182.7 0.2 copy.25
  182.9 0.3 concatenate.37
  183.2 2.0 collective-permute-done.2
  185.3 0.2 copy.26
  185.5 0.3 concatenate.39
  185.9 5.9 %fusion.7 = f32[2,128,32,16]{1,3,0,2:T(8,128)S(1)} fusion(f32[32,128,256,1]{2,1,0,3:T(8,128)} %bitcast.65, f32[2,128,32,16]{1,3,0,2:T(8,128)S(1)} %copy.28, f32[2,128,32,16]{1,3,0,2:T(8,128)S(1)} %copy.27), kind=kOutput, calls=%fused_computation.8 | convolution fusion | flops 402915328 | bytes 5767168 | tf_op jit(solution)/shard_map/gts,bsgc->btgc/dot_general | solution.py:42
  191.8 0.3 copy.29
  192.1 0.9 fusion.14
  193.0 0.3 concatenate.34
  193.3 0.3 concatenate.33
  193.6 0.1 copy_dynamic-update-slice_fusion.1
  193.6 0.1 copy_dynamic-update-slice_fusion
  193.7 5.9 %fusion.4 = f32[2,128,32,16]{1,3,0,2:T(8,128)S(1)} fusion(f32[2,256,32,16]{1,3,0,2:T(8,128)S(1)} %copy_dynamic-update-slice_fusion, f32[32,128,256,1]{2,1,0,3:T(8,128)} %bitcast.64), kind=kOutput, calls=%fused_computation.7 | convolution fusion | flops 402653184 | bytes 5767168 | tf_op jit(solution)/shard_map/gts,bsgc->btgc/dot_general | solution.py:42
  199.7 0.3 copy.21
  200.0 0.2 copy.22
  200.2 0.8 fusion.16
  201.0 0.1 copy.23
  201.2 0.4 stack.2
  201.6 95.5 %all_to_all.5 = bf16[16,256,512]{1,2,0:T(8,128)(2,1)S(1)} all-to-all(bf16[16,256,512]{1,2,0:T(8,128)(2,1)S(1)} %stack.2), channel_id=1, replica_groups=mesh['row'=16,'col'=16] {'col'}, dimensions={0} | all-to-all | bytes 8388608 | tf_op jit(solution)/shard_map/all_to_all | solution.py:63
  297.1 2.1 copy-done.1
  299.1 5.6 %convolution_convert_fusion = bf16[8192,512]{1,0:T(8,128)(2,1)} fusion(bf16[256,8192]{0,1:T(8,128)(2,1)S(1)} %bitcast.60, bf16[256,512]{1,0:T(8,128)(2,1)S(1)} %copy-done), kind=kOutput, calls=%fused_computation | convolution fusion | flops 2151677952 | bytes 12845056 | tf_op jit(solution)/shard_map/dot_general | solution.py:95
  304.7 0.0 reduce-scatter.5.cloned.1.call-update
  304.8 3.5 fusion.18
  308.3 2.4 copy.40
  310.7 2.3 concatenate.42
  313.0 8.2 %reshape.71 = f32[32,128,257]{2,1,0:T(8,128)} reshape(f32[32,32896]{1,0:T(8,128)} %concatenate.42) | data formatting | bytes 8421376 | tf_op jit(solution)/shard_map/reshape | solution.py:91
  321.2 3.2 slice_reduce_fusion
  324.4 0.1 rev.7
  324.5 0.8 copy.31
  325.3 0.8 copy.32
  326.2 61.5 %psum.7 = f32[32,128]{1,0:T(8,128)S(1)} all-reduce(f32[32,128]{1,0:T(8,128)S(1)} %rev.7), channel_id=1, replica_groups=mesh['row'=16,'col'=16] {'row'}, use_global_device_ids=true, to_apply=%region_3.0 | all-reduce | flops 4096 | bytes 32768 | tf_op jit(solution)/shard_map/psum | solution.py:93
  387.7 0.6 broadcast_multiply_fusion
  388.3 7.7 %convolution_convert_fusion.2 = bf16[256,512]{1,0:T(8,128)(2,1)} fusion(bf16[256,8192]{0,1:T(8,128)(2,1)} %bitcast.61, bf16[8192,512]{1,0:T(8,128)(2,1)} %all-gather.2.cloned.1.call-done), kind=kOutput, calls=%fused_computation.9 | convolution fusion | flops 2147614720 | bytes 12845056 | tf_op jit(solution)/shard_map/dot_general | solution.py:66
  396.0 19.7 %reduce-scatter.5.cloned.1.call-done = bf16[512,512]{1,0:T(8,128)(2,1)} async-done(((bf16[8192,512]{1,0:T(8,128)(2,1)}), bf16[512,512]{1,0:T(8,128)(2,1)}) %reduce-scatter.5.cloned.1.call-update) | async-done | bytes 524304 | tf_op jit(solution)/shard_map/reduce_scatter | solution.py:94
  415.7 1.9 multiply_convert_fusion
  (30 shorter events, 0.3 us)
Async XLA Ops:
  7.2 83.1 %copy-start = (bf16[256,512]{1,0:T(8,128)(2,1)S(1)}, bf16[256,512]{1,0:T(8,128)(2,1)}, u32[]{:S(2)}) copy-start(bf16[256,512]{1,0:T(8,128)(2,1)} %param.11) | copy-start | bytes 786436
  7.2 83.1 %all-gather.2.cloned.1.call-start = ((), (), s32[]{:S(2)}) async-start(), calls=%async_computation.3 | async-start | bytes 8912896 | tf_op jit(solution)/shard_map/all_gather | solution.py:65
  7.9 170.9 %reduce-scatter.3.cloned.1.call-start = ((), (), s32[]{:S(2)}) async-start(), calls=%async_computation.4 | async-start | bytes 4456448 | tf_op jit(solution)/shard_map/reduce_scatter | solution.py:71
  98.0 0.9 copy-start.6
  98.0 3.3 copy-start.7
  98.0 5.7 %copy-start.8 = (f32[32,128]{1,0:T(8,128)S(1)}, f32[32,128]{1,0:T(8,128)}, u32[]{:S(2)}) copy-start(f32[32,128]{1,0:T(8,128)} %param.9) | copy-start | bytes 49156
  98.1 317.7 %reduce-scatter.5.cloned.1.call-start = ((), (), s32[]{:S(2)}) async-start(), calls=%async_computation.5 | async-start | bytes 8912896 | tf_op jit(solution)/shard_map/reduce_scatter | solution.py:94
  99.1 83.5 %collective-permute-start = (bf16[128,512]{0,1:T(8,128)(2,1)S(1)}, bf16[128,512]{0,1:T(8,128)(2,1)S(1)}, u32[]{:S(2)}, u32[]{:S(2)}) collective-permute-start(bf16[128,512]{0,1:T(8,128)(2,1)S(1)} %slice.34), channel_id=1, source_target_pairs={{0,16},{16,32},{32,48},{48,64},{64,80},{80,96},{96,112},{112,128},... | collective-permute-start | bytes 393224 | tf_op jit(solution)/shard_map/ppermute | solution.py:11
  101.5 81.2 %collective-permute-start.1 = (bf16[128,512]{0,1:T(8,128)(2,1)S(1)}, bf16[128,512]{0,1:T(8,128)(2,1)S(1)}, u32[]{:S(2)}, u32[]{:S(2)}) collective-permute-start(bf16[128,512]{0,1:T(8,128)(2,1)S(1)} %slice.35), channel_id=1, source_target_pairs={{0,16},{16,32},{32,48},{48,64},{64,80},{80,96},{96,112},{112,128},... | collective-permute-start | bytes 393224 | tf_op jit(solution)/shard_map/ppermute | solution.py:11
  113.6 2.2 slice-start
  129.1 2.2 slice-start.1
  131.3 47.5 %copy-start.2 = (bf16[256,512]{1,0:T(8,128)(2,1)S(1)}, bf16[256,512]{1,0:T(8,128)(2,1)}, u32[]{:S(2)}) copy-start(bf16[256,512]{1,0:T(8,128)(2,1)} %param.6) | copy-start | bytes 786436
  180.5 4.7 %collective-permute-start.2 = (bf16[128,512]{1,0:T(8,128)(2,1)}, bf16[128,512]{1,0:T(8,128)(2,1)S(1)}, u32[]{:S(2)}, u32[]{:S(2)}) collective-permute-start(bf16[128,512]{1,0:T(8,128)(2,1)} %slice.42), channel_id=1, source_target_pairs={{16,0},{32,16},{48,32},{64,48},{80,64},{96,80},{112,96},{128,112},... | collective-permute-start | bytes 393224 | tf_op jit(solution)/shard_map/ppermute | solution.py:11
  193.7 6.5 %copy-start.3 = (bf16[256,512]{1,0:T(8,128)(2,1)S(1)}, bf16[256,512]{1,0:T(8,128)(2,1)}, u32[]{:S(2)}) copy-start(bf16[256,512]{1,0:T(8,128)(2,1)} %reduce-scatter.3.cloned.1.call-done) | copy-start | bytes 786436
  297.1 2.1 copy-start.1
  313.0 11.5 %copy-start.5 = (bf16[256,512]{0,1:T(8,128)(2,1)S(1)}, bf16[256,512]{0,1:T(8,128)(2,1)}, u32[]{:S(2)}) copy-start(bf16[256,512]{0,1:T(8,128)(2,1)} %get-tuple-element.13) | copy-start | bytes 786436
  313.0 12.3 %copy-start.4 = (bf16[256,512]{0,1:T(8,128)(2,1)S(1)}, bf16[256,512]{0,1:T(8,128)(2,1)}, u32[]{:S(2)}) copy-start(bf16[256,512]{0,1:T(8,128)(2,1)} %get-tuple-element.12) | copy-start | bytes 786436
Sparse Core Ops, SparseCore 0:
  10.7 79.5 all-gather.1
  98.2 80.5 reduce-scatter.2
  304.9 110.8 reduce-scatter.4
